TPU v7x, 512 devices: a whole 4x4x16 slice. The times are simulated.
512 devices in a mesh: seq: 64 (over z, x), head: 8 (over y, core).
Axes of the slice: x: 4, y: 4, z: 16, core: 2. Of those that a mesh axis runs over, the one named last changes fastest.
Arguments:
- tokens: bfloat16 [65536, 1024], P('seq'), may hold values from -60 to 60
- qkv_weight: bfloat16 [1024, 8, 384], P(None, 'head'), may hold values from -0.1875 to 0.1875
- out_weight: bfloat16 [8, 128, 1024], P('head'), may hold values from -0.1875 to 0.1875
- members: int32 [8, 256, 768], P('head', None, 'seq'), may hold values from 0 to 65535, as said below
- counts: int32 [8, 64, 256], P('head', 'seq'), may hold values from 1 to 12, as said below
Outputs:
- mixed: bfloat16 [65536, 1024], P(('seq', 'head'))
- centroids: float32 [8, 256, 128], P('head', 'seq')
Inputs may be any that keep to these rules, and one draw needn't show every extreme that they name: `members`: the entries of slots j of any cluster lie in slab j // 12, i.e. in positions 1024 * (j // 12) up to 1024 * (j // 12 + 1) - 1. For each head and slab, the valid entries (j % 12 < counts) over all clusters name every token of that slab exactly once; the other entries are padding with some position of the same slab. For each head and slab the counts over the 256 clusters sum to 1024. For each head, one cluster has 12 members from every slab. Split the 256 clusters into 64 aligned groups of equal size; for each head and slab the counts of one group sum to at most 32, and exactly 32 for the group that holds the full cluster.
All inputs are finite; a program needn't handle non-finite values.
Results may differ from a plain program's by a relative error of at most 0.02.
The roundings to bfloat16 on the way count: a program that leaves them out, or rounds other values in their place, can miss the bound.
Values may be sent and summed in bfloat16 or wider, within the bound.
A program may use at most 128 MiB of HBM per device.

v0:
```python
import jax
import jax.numpy as jnp
from jax import lax
from jax.sharding import PartitionSpec as P

eps_norm = 1e-06


def unit_rows(keys_in):
    widened = keys_in.astype(jnp.float32)
    return widened * lax.rsqrt(jnp.sum(widened * widened, axis=-1, keepdims=True) + eps_norm)


def normalize_rows(sums):
    return sums * lax.rsqrt(jnp.mean(sums * sums, axis=-1, keepdims=True) + eps_norm)


def attend_core(got_rows, got_positions, head_dim, scale):
    seq_count = got_positions.shape[1]
    slab_slots = got_positions.shape[3]
    same_slot = jnp.eye(seq_count * slab_slots, dtype=bool).reshape(
        seq_count, slab_slots, seq_count, slab_slots
    )
    queries = got_rows[..., :head_dim]
    keys_in = got_rows[..., head_dim : 2 * head_dim]
    values_in = got_rows[..., 2 * head_dim :]
    scores = (
        jnp.einsum("hscie,htcje->hcsitj", queries, keys_in, preferred_element_type=jnp.float32)
        * scale
    )
    ordered = jnp.transpose(got_positions, (0, 2, 1, 3))
    query_pos = ordered[:, :, :, :, None, None]
    key_pos = ordered[:, :, None, None, :, :]
    allowed = (key_pos >= 0) & (key_pos <= query_pos) | same_slot[None, None]
    masked = jnp.where(allowed, scores, -1e30)
    highest = jnp.max(masked, axis=(4, 5), keepdims=True)
    expo = jnp.exp(masked - highest)
    probs = (expo / jnp.sum(expo, axis=(4, 5), keepdims=True)).astype(jnp.bfloat16)
    return jnp.einsum(
        "hcsitj,htcje->hscie", probs, values_in, preferred_element_type=jnp.float32
    ).astype(jnp.bfloat16)


def on_device(tokens, qkv_weight, out_weight, members, counts):
    slab_len = tokens.shape[0]
    heads_here = qkv_weight.shape[1]
    head_dim = out_weight.shape[1]
    clusters = members.shape[1]
    slab_slots = members.shape[2]
    seq_count = lax.axis_size("seq")
    owned = clusters // seq_count
    my_slab = lax.axis_index("seq")
    scale = head_dim ** (-0.5)
    projected = jnp.einsum(
        "td,dhe->hte", tokens, qkv_weight, preferred_element_type=jnp.float32
    ).astype(jnp.bfloat16)
    local_ids = members - my_slab * slab_len
    valid = jnp.arange(slab_slots, dtype=jnp.int32)[None, None, :] < counts[:, 0, :, None]
    positions = jnp.where(valid, members, -1)
    member_rows = jax.vmap(lambda table, index: table[index])(projected, local_ids)
    slab_sums = jnp.sum(
        jnp.where(valid[..., None], unit_rows(member_rows[..., head_dim : 2 * head_dim]), 0.0),
        axis=2,
    )
    all_sums = lax.psum(slab_sums, "seq")
    mine = lax.dynamic_slice_in_dim(all_sums, my_slab * owned, owned, 1)
    head_index = jnp.arange(heads_here, dtype=jnp.int32)[:, None, None]
    send_rows = member_rows.reshape(heads_here, seq_count, owned, slab_slots, 3 * head_dim)
    send_positions = positions.reshape(heads_here, seq_count, owned, slab_slots)
    got_rows = lax.all_to_all(send_rows, "seq", split_axis=1, concat_axis=1, tiled=True)
    got_positions = lax.all_to_all(send_positions, "seq", split_axis=1, concat_axis=1, tiled=True)
    attended = attend_core(got_rows, got_positions, head_dim, scale)
    answered = lax.all_to_all(attended, "seq", split_axis=1, concat_axis=1, tiled=True)
    result = answered
    answered = result
    answered = answered.reshape(heads_here, clusters, slab_slots, head_dim)
    target = jnp.where(valid, local_ids, slab_len)
    head_out = (
        jnp.zeros((slab_len, heads_here, head_dim), jnp.bfloat16)
        .at[target, head_index]
        .set(answered, mode="drop")
    )
    centroids = normalize_rows(mine)
    all_heads = lax.all_to_all(head_out, "head", split_axis=0, concat_axis=1, tiled=True)
    mixed = jnp.einsum(
        "the,heo->to",
        all_heads,
        lax.all_gather(out_weight, "head", axis=0, tiled=True),
        preferred_element_type=jnp.float32,
    )
    return (mixed.astype(jnp.bfloat16), centroids)


def solution(mesh):
    return jax.shard_map(
        on_device,
        mesh=mesh,
        in_specs=(
            P("seq", None),
            P(None, "head", None),
            P("head", None, None),
            P("head", None, "seq"),
            P("head", "seq", None),
        ),
        out_specs=(P(("seq", "head"), None), P("head", "seq", None)),
        check_vma=False,
    )
```

profile of v0, /device:TPU:1, one launch (start us, length us, event | category | flops | bytes accessed | tf_op | source)
XLA Modules:
  0.0 421.6 jit_solution(6526205904434901323)
XLA Ops:
  8.0 0.0 copy-start
  8.0 0.9 compare_select_fusion.2
  8.9 0.8 copy.53
  9.7 19.1 %all-to-all-start.1 = ((s32[1,64,4,12]{3,2,0,1:T(4,128)}), s32[1,64,4,12]{3,2,0,1:T(4,128)S(1)}, u32[]{:S(2)}, u32[]{:S(2)}) async-start(s32[1,64,4,12]{3,2,0,1:T(4,128)} %bitcast.10), calls=%async_computation.1 | async-start | bytes 262144 | tf_op jit(solution)/shard_map/all_to_all | solution.py:71
  28.8 0.0 copy-done
  28.8 3.0 fusion.5
  31.9 0.1 copy.49
  32.0 0.1 reshape.198
  32.2 1.5 copy.50
  33.7 29.1 %gather_fusion = bf16[3072,384]{1,0:T(8,128)(2,1)} fusion(bf16[1,1024,384]{2,1,0:T(8,128)(2,1)S(1)} %copy.50, s32[3072]{0:T(1024)S(1)} %reshape.198), kind=kCustom, calls=%fused_computation | custom fusion | bytes 4743168 | tf_op jit(solution)/shard_map/vmap()/gather | solution.py:60
  62.8 5.0 %reshape.180 = bf16[1,64,4,12,384]{4,3,2,1,0:T(8,128)(2,1)} reshape(bf16[3072,384]{1,0:T(8,128)(2,1)} %gather_fusion) | data formatting | bytes 4718592 | tf_op jit(solution)/shard_map/reshape | solution.py:68
  67.8 4.2 copy.51
  72.0 0.0 all-to-all-done.1
  72.0 14.8 %all-to-all-start = ((bf16[1,64,4,12,384]{4,2,3,0,1:T(4,128)(2,1)}), bf16[1,64,4,12,384]{4,2,3,0,1:T(4,128)(2,1)}, u32[]{:S(2)}, u32[]{:S(2)}) async-start(bf16[1,64,4,12,384]{4,2,3,0,1:T(4,128)(2,1)} %copy.51), calls=%async_computation | async-start | bytes 4718592 | tf_op jit(solution)/shard_map/all_to_all | solution.py:70
  86.7 0.0 copy-start.3
  86.7 0.0 all-reduce.3.cloned.1.call-start
  86.8 5.0 %reshape.197 = bf16[1,256,12,384]{3,2,1,0:T(8,128)(2,1)} reshape(bf16[3072,384]{1,0:T(8,128)(2,1)} %gather_fusion) | data formatting | bytes 4718592 | tf_op jit(solution)/shard_map/vmap()/gather | solution.py:60
  91.8 1.8 fusion.2
  93.6 0.0 copy-done.3
  93.6 0.1 iota_compare_fusion
  93.8 3.7 fusion.4
  97.5 0.0 all-reduce.3.cloned.1.call-update
  97.5 0.2 all-gather.2.cloned.1.call-start
  97.8 0.3 all-gather.2.cloned.1.call-update
  98.1 1.8 broadcast_compare_fusion
  100.0 0.1 copy.56
  100.1 0.1 broadcast_compare_fusion.1
  100.1 0.1 copy.55
  100.2 0.0 copy-start.1
  100.2 93.1 %all-to-all-done = bf16[1,64,4,12,384]{4,2,3,0,1:T(4,128)(2,1)} async-done(((bf16[1,64,4,12,384]{4,2,3,0,1:T(4,128)(2,1)}), bf16[1,64,4,12,384]{4,2,3,0,1:T(4,128)(2,1)}, u32[]{:S(2)}, u32[]{:S(2)}) %all-to-all-start) | async-done | bytes 2359328 | tf_op jit(solution)/shard_map/all_to_all | solution.py:70
  193.3 3.3 fusion.16
  196.6 0.0 copy-done.1
  196.6 10.4 %fusion.17 = (f32[4,64,12]{1,2,0:T(8,128)S(1)}, f32[4,64,12,64,12]{1,3,4,2,0:T(8,128)}) fusion(bf16[1,64,4,12,128]{4,2,3,0,1:T(4,128)(2,1)S(1)} %get-tuple-element.4, bf16[1,64,4,12,128]{4,2,3,0,1:T(4,128)(2,1)S(1)} %get-tuple-element.3, pred[64,12,64,12]{0,2,3,1:T(8,128)(4,1)S(1)} %copy-done.1, s32[4,64,12]{1,2,0:T(8,128)S(1)} %copy.56, ...), kind=kOutput, calls=%fused_computation.48 | convolution fusion | flops 618132480 | bytes 11627520 | tf_op jit(solution)/shard_map/hscie,htcje->hcsitj/dot_general | solution.py:28
  207.0 0.0 copy-start.2
  207.0 10.2 %fusion = f32[4,64,12]{1,2,0:T(8,128)S(1)} fusion(f32[4,64,12,64,12]{1,3,4,2,0:T(8,128)} %get-tuple-element.9, f32[4,64,12]{1,2,0:T(8,128)S(1)} %get-tuple-element.8), kind=kLoop, calls=%fused_computation.5 | loop fusion | flops 4715520 | bytes 9461760 | tf_op jit(solution)/shard_map/reduce_sum | solution.py:38
  217.2 0.0 copy-done.2
  217.2 8.5 %fusion.6 = bf16[1,64,4,12,128]{4,1,3,2,0:T(8,128)(2,1)S(1)} fusion(f32[4,64,12,64,12]{1,3,4,2,0:T(8,128)} %get-tuple-element.9, f32[4,64,12]{1,2,0:T(8,128)S(1)} %fusion, f32[4,64,12]{1,2,0:T(8,128)S(1)} %get-tuple-element.8, bf16[1,64,4,12,128]{4,2,3,0,1:T(4,128)(2,1)S(1)} %copy-done.2), kind=kOutput, calls=%fused_computation.16 | convolution fusion | flops 611450880 | bytes 11034624 | tf_op jit(solution)/shard_map/hcsitj,htcje->hscie/dot_general | solution.py:39
  225.7 0.0 copy-start.4
  225.7 0.0 copy-start.5
  225.8 1.5 copy.61
  227.3 11.4 %all-to-all-start.2 = ((bf16[1,64,4,12,128]{4,2,3,0,1:T(4,128)(2,1)}), bf16[1,64,4,12,128]{4,2,3,0,1:T(4,128)(2,1)}, u32[]{:S(2)}, u32[]{:S(2)}) async-start(bf16[1,64,4,12,128]{4,2,3,0,1:T(4,128)(2,1)} %copy.61), calls=%async_computation.2 | async-start | bytes 1572864 | tf_op jit(solution)/shard_map/all_to_all | solution.py:73
  238.7 0.0 copy-done.4
  238.7 0.1 multiply_reduce_fusion
  238.8 0.0 copy-done.5
  238.8 0.1 and_reduce_fusion
  238.9 0.1 copy.48
  239.0 0.1 reshape.206
  239.2 136.0 %all-reduce.3.cloned.1.call-done = f32[1,256,128]{2,1,0:T(8,128)} async-done(((f32[1,256,128]{2,1,0:T(8,128)}), f32[1,256,128]{2,1,0:T(8,128)}) %all-reduce.3.cloned.1.call-update) | async-done | bytes 131088 | tf_op jit(solution)/shard_map/psum | solution.py:65
  375.2 0.8 multiply_reduce_fusion.1
  376.0 0.0 all-to-all-done.2
  376.0 1.4 copy.62
  377.4 1.1 reshape.208
  378.4 8.6 %scatter_custom_fusion = bf16[1024,128]{1,0:T(8,128)(2,1)S(1)} fusion(s32[3072]{0:T(1024)S(1)} %reshape.206, bf16[3072,128]{1,0:T(8,128)(2,1)} %reshape.208, bf16[]{:T(256)} %constant.15.clone.1), kind=kCustom, calls=%fused_computation.23 | custom fusion | bytes 262656
  387.1 0.5 broadcast.148
  387.6 0.8 reduce.13
  388.4 0.8 reshape.225
  389.2 15.4 %all-to-all-start.3 = ((bf16[8,2,8192]{2,1,0:T(2,128)(2,1)}), bf16[8,2,8192]{2,1,0:T(2,128)(2,1)S(1)}, u32[]{:S(2)}, u32[]{:S(2)}) async-start(bf16[8,2,8192]{2,1,0:T(2,128)(2,1)} %reshape.225), calls=%async_computation.3 | async-start | bytes 524288 | tf_op jit(solution)/shard_map/all_to_all | solution.py:84
  404.6 1.3 dynamic-slice_multiply_fusion
  405.9 5.2 %all-to-all-done.3 = bf16[8,2,8192]{2,1,0:T(2,128)(2,1)S(1)} async-done(((bf16[8,2,8192]{2,1,0:T(2,128)(2,1)}), bf16[8,2,8192]{2,1,0:T(2,128)(2,1)S(1)}, u32[]{:S(2)}, u32[]{:S(2)}) %all-to-all-start.3) | async-done | bytes 262176 | tf_op jit(solution)/shard_map/all_to_all | solution.py:84
  411.1 0.3 reshape.226
  411.4 0.0 all-gather.2.cloned.1.call-done
  411.4 2.7 fusion.7
  (7 shorter events, 0.1 us)
Async XLA Ops:
  8.0 20.8 %copy-start = (bf16[1024,1024]{1,0:T(8,128)(2,1)S(1)}, bf16[1024,1024]{1,0:T(8,128)(2,1)}, u32[]{:S(2)}) copy-start(bf16[1024,1024]{1,0:T(8,128)(2,1)} %param.5) | copy-start | bytes 6291460
  9.7 62.3 %all-to-all-start.1 = ((s32[1,64,4,12]{3,2,0,1:T(4,128)}), s32[1,64,4,12]{3,2,0,1:T(4,128)S(1)}, u32[]{:S(2)}, u32[]{:S(2)}) async-start(s32[1,64,4,12]{3,2,0,1:T(4,128)} %bitcast.10), calls=%async_computation.1 | async-start | bytes 262144 | tf_op jit(solution)/shard_map/all_to_all | solution.py:71
  72.0 121.4 %all-to-all-start = ((bf16[1,64,4,12,384]{4,2,3,0,1:T(4,128)(2,1)}), bf16[1,64,4,12,384]{4,2,3,0,1:T(4,128)(2,1)}, u32[]{:S(2)}, u32[]{:S(2)}) async-start(bf16[1,64,4,12,384]{4,2,3,0,1:T(4,128)(2,1)} %copy.51), calls=%async_computation | async-start | bytes 4718592 | tf_op jit(solution)/shard_map/all_to_all | solution.py:70
  86.7 6.9 %copy-start.3 = (s32[1,1,256]{2,1,0:T(1,128)S(1)}, s32[1,1,256]{2,1,0:T(1,128)}, u32[]{:S(2)}) copy-start(s32[1,1,256]{2,1,0:T(1,128)} %param.9) | copy-start | bytes 3076
  86.7 288.4 %all-reduce.3.cloned.1.call-start = ((), (), s32[]{:S(2)}) async-start(), calls=%async_computation.5 | async-start | bytes 262144 | tf_op jit(solution)/shard_map/psum | solution.py:65
  97.5 313.9 %all-gather.2.cloned.1.call-start = ((), (), s32[]{:S(2)}) async-start(), calls=%async_computation.4 | async-start | bytes 2359296 | tf_op jit(solution)/shard_map/all_gather | solution.py:88
  100.2 96.4 %copy-start.1 = (pred[64,12,64,12]{0,2,3,1:T(8,128)(4,1)S(1)}, pred[64,12,64,12]{0,2,3,1:T(8,128)(4,1)}, u32[]{:S(2)}) copy-start(pred[64,12,64,12]{0,2,3,1:T(8,128)(4,1)} %broadcast_compare_fusion) | copy-start | bytes 1769476
  207.0 10.2 %copy-start.2 = (bf16[1,64,4,12,128]{4,2,3,0,1:T(4,128)(2,1)S(1)}, bf16[1,64,4,12,128]{4,2,3,0,1:T(4,128)(2,1)}, u32[]{:S(2)}) copy-start(bf16[1,64,4,12,128]{4,2,3,0,1:T(4,128)(2,1)} %get-tuple-element.2) | copy-start | bytes 2359300
  225.7 12.9 %copy-start.4 = (s32[2]{0:T(128)S(1)}, s32[2]{0:T(128)}, u32[]{:S(2)}) copy-start(s32[2]{0:T(128)} %constant.45) | copy-start | bytes 28
  225.7 13.0 %copy-start.5 = (s32[2]{0:T(128)S(1)}, s32[2]{0:T(128)}, u32[]{:S(2)}) copy-start(s32[2]{0:T(128)} %constant.48) | copy-start | bytes 28
  227.3 148.7 %all-to-all-start.2 = ((bf16[1,64,4,12,128]{4,2,3,0,1:T(4,128)(2,1)}), bf16[1,64,4,12,128]{4,2,3,0,1:T(4,128)(2,1)}, u32[]{:S(2)}, u32[]{:S(2)}) async-start(bf16[1,64,4,12,128]{4,2,3,0,1:T(4,128)(2,1)} %copy.61), calls=%async_computation.2 | async-start | bytes 1572864 | tf_op jit(solution)/shard_map/all_to_all | solution.py:73
  389.2 21.9 %all-to-all-start.3 = ((bf16[8,2,8192]{2,1,0:T(2,128)(2,1)}), bf16[8,2,8192]{2,1,0:T(2,128)(2,1)S(1)}, u32[]{:S(2)}, u32[]{:S(2)}) async-start(bf16[8,2,8192]{2,1,0:T(2,128)(2,1)} %reshape.225), calls=%async_computation.3 | async-start | bytes 524288 | tf_op jit(solution)/shard_map/all_to_all | solution.py:84
Sparse Core Ops, SparseCore 0:
  97.6 277.4 all-reduce.2
Sparse Core Ops, SparseCore 1:
  100.1 35.2 all-gather.1
where the time goes:
time: 423 us; the launch traced here: 422 us
  waiting for transfers between devices  235 us (56%)
  local copies, waits for them, and re-layouts  63.8 us (15%)
  starting transfers between devices  60.9 us (14%)
  matrix products  24.6 us (6%)
  other arithmetic  21.9 us (5%)
  between operations  15.7 us (4%)
    psum x1, waiting for transfers between devices, on_device(): all_sums = lax.psum(slab_sums, 'seq')  136 us
    all_to_all x1, waiting for transfers between devices, on_device(): lax.all_to_all(send_rows, 'seq', split_axis=1, concat_axis=1, tiled=True)  93.1 us
    gather x4, local copies, waits for them, and re-layouts, on_device(): table[index]  34.3 us
    all_to_all x1, starting transfers between devices, on_device(): lax.all_to_all(send_positions, 'seq', split_axis=1, concat_axis=1, tiled=...  19.1 us
    all_to_all x1, starting transfers between devices, on_device(): lax.all_to_all(head_out, 'head', split_axis=0, concat_axis=1, tiled=True)  15.4 us
    all_to_all x1, starting transfers between devices, on_device(): lax.all_to_all(send_rows, 'seq', split_axis=1, concat_axis=1, tiled=True)  14.8 us
    all_to_all x1, starting transfers between devices, on_device(): lax.all_to_all(attended, 'seq', split_axis=1, concat_axis=1, tiled=True)  11.4 us
    dot_general x1, matrix products, attend_core(): jnp.einsum('hscie,htcje->hcsitj', queries, keys_in, preferred_element_typ...  10.4 us
  transfers between devices with their start and end apart: 6, of which 3 were waited for; matrix products, arithmetic and copies ran while one was open for 25% of the time, Pallas kernels for 0%

commit v1 on v0

--- a/solution.py
+++ b/solution.py
@@ -4,6 +4,12 @@
 from jax.sharding import PartitionSpec as P
 
 eps_norm = 1e-06
+
+
+def summed_here(block, name):
+    parts = lax.all_gather(block, name, axis=0, tiled=False)
+    total = parts.sum(axis=0)
+    return total
 
 
 def unit_rows(keys_in):
@@ -62,7 +68,7 @@
         jnp.where(valid[..., None], unit_rows(member_rows[..., head_dim : 2 * head_dim]), 0.0),
         axis=2,
     )
-    all_sums = lax.psum(slab_sums, "seq")
+    all_sums = summed_here(slab_sums, "seq")
     mine = lax.dynamic_slice_in_dim(all_sums, my_slab * owned, owned, 1)
     head_index = jnp.arange(heads_here, dtype=jnp.int32)[:, None, None]
     send_rows = member_rows.reshape(heads_here, seq_count, owned, slab_slots, 3 * head_dim)

time: 423 us -> 342 us (0.81)
  waiting for transfers between devices: 235 us -> 162 us
  starting transfers between devices: 60.9 us -> 51.7 us
    psum x1 -> x0, waiting for transfers between devices: 136 us -> none  [on_device(): all_sums = lax.psum(slab_sums, 'seq')]
    all_to_all x1, waiting for transfers between devices: 0.01 us -> 51.4 us  [on_device(): lax.all_to_all(attended, 'seq', split_axis=1, concat_axis=1, tiled=True)]
    all_to_all x1, waiting for transfers between devices: 93.1 us -> 103 us  [on_device(): lax.all_to_all(send_rows, 'seq', split_axis=1, concat_axis=1, tiled=True)]
    all_to_all x1, starting transfers between devices: 15.4 us -> 5.99 us  [on_device(): lax.all_to_all(head_out, 'head', split_axis=0, concat_axis=1, tiled=True)]
  transfers between devices with their start and end apart: 6 -> 6, of which waited for: 3 -> 3; matrix products, arithmetic and copies ran while one was open for 25% -> 32% of each run, Pallas kernels for 0% -> 0%
where the time goes in v1:
time: 342 us; the launch traced here: 341 us
  waiting for transfers between devices  162 us (47%)
  local copies, waits for them, and re-layouts  63.8 us (19%)
  starting transfers between devices  51.7 us (15%)
  matrix products  24.9 us (7%)
  other arithmetic  24.3 us (7%)
  between operations  14.3 us (4%)
    all_to_all x1, waiting for transfers between devices, on_device(): lax.all_to_all(send_rows, 'seq', split_axis=1, concat_axis=1, tiled=True)  103 us
    all_to_all x1, waiting for transfers between devices, on_device(): lax.all_to_all(attended, 'seq', split_axis=1, concat_axis=1, tiled=True)  51.4 us
    gather x4, local copies, waits for them, and re-layouts, on_device(): table[index]  34.3 us
    all_to_all x1, starting transfers between devices, on_device(): lax.all_to_all(send_positions, 'seq', split_axis=1, concat_axis=1, tiled=...  19.1 us
    all_to_all x1, starting transfers between devices, on_device(): lax.all_to_all(send_rows, 'seq', split_axis=1, concat_axis=1, tiled=True)  14.7 us
    all_to_all x1, starting transfers between devices, on_device(): lax.all_to_all(attended, 'seq', split_axis=1, concat_axis=1, tiled=True)  11.6 us
    dot_general x1, matrix products, attend_core(): jnp.einsum('hscie,htcje->hcsitj', queries, keys_in, preferred_element_typ...  10.4 us
    reduce_sum x1, other arithmetic, attend_core(): jnp.sum(expo, axis=(4, 5), keepdims=True)  10.3 us
  transfers between devices with their start and end apart: 6, of which 3 were waited for; matrix products, arithmetic and copies ran while one was open for 32% of the time, Pallas kernels for 0%

profile of v1, /device:TPU:1, one launch (start us, length us, event | category | flops | bytes accessed | tf_op | source)
XLA Modules:
  0.0 340.5 jit_solution(10861600883006723776)
XLA Ops:
  7.2 0.0 copy-start
  7.2 0.0 all-gather.4.cloned.1.call-start
  7.2 0.7 all-gather.4.cloned.1.call-update
  7.9 0.7 compare_select_fusion.2
  8.7 0.8 copy.69
  9.4 19.1 %all-to-all-start.1 = ((s32[1,64,4,12]{3,2,0,1:T(4,128)}), s32[1,64,4,12]{3,2,0,1:T(4,128)S(1)}, u32[]{:S(2)}, u32[]{:S(2)}) async-start(s32[1,64,4,12]{3,2,0,1:T(4,128)} %bitcast.10), calls=%async_computation.1 | async-start | bytes 262144 | tf_op jit(solution)/shard_map/all_to_all | solution.py:77
  28.6 0.0 copy-done
  28.6 3.0 fusion.5
  31.7 0.1 copy.65
  31.8 0.1 reshape.204
  31.9 1.5 copy.66
  33.5 29.1 %gather_fusion = bf16[3072,384]{1,0:T(8,128)(2,1)} fusion(bf16[1,1024,384]{2,1,0:T(8,128)(2,1)S(1)} %copy.66, s32[3072]{0:T(1024)S(1)} %reshape.204), kind=kCustom, calls=%fused_computation | custom fusion | bytes 4743168 | tf_op jit(solution)/shard_map/vmap()/gather | solution.py:66
  62.6 5.0 %reshape.186 = bf16[1,64,4,12,384]{4,3,2,1,0:T(8,128)(2,1)} reshape(bf16[3072,384]{1,0:T(8,128)(2,1)} %gather_fusion) | data formatting | bytes 4718592 | tf_op jit(solution)/shard_map/reshape | solution.py:74
  67.5 4.2 %copy.67 = bf16[1,64,4,12,384]{4,2,3,0,1:T(4,128)(2,1)} copy(bf16[1,64,4,12,384]{4,3,2,1,0:T(8,128)(2,1)} %reshape.186) | data formatting | bytes 4718592 | tf_op jit(solution)/shard_map/reshape | solution.py:74
  71.8 0.0 all-to-all-done.1
  71.8 14.7 %all-to-all-start = ((bf16[1,64,4,12,384]{4,2,3,0,1:T(4,128)(2,1)}), bf16[1,64,4,12,384]{4,2,3,0,1:T(4,128)(2,1)}, u32[]{:S(2)}, u32[]{:S(2)}) async-start(bf16[1,64,4,12,384]{4,2,3,0,1:T(4,128)(2,1)} %copy.67), calls=%async_computation | async-start | bytes 4718592 | tf_op jit(solution)/shard_map/all_to_all | solution.py:76
  86.5 0.0 copy-start.3
  86.5 0.2 all-gather.6.cloned.1.call-start
  86.7 5.0 %reshape.203 = bf16[1,256,12,384]{3,2,1,0:T(8,128)(2,1)} reshape(bf16[3072,384]{1,0:T(8,128)(2,1)} %gather_fusion) | data formatting | bytes 4718592 | tf_op jit(solution)/shard_map/vmap()/gather | solution.py:66
  91.7 1.8 fusion.2
  93.6 0.0 copy-done.3
  93.6 0.1 iota_compare_fusion
  93.7 3.7 %fusion.4 = f32[256,128]{1,0:T(8,128)} fusion(f32[256,12]{1,0:T(8,128)S(1)} %add_rsqrt_fusion, pred[256,12]{1,0:T(8,128)(4,1)S(1)} %iota_compare_fusion, bf16[1,256,12,384]{3,2,1,0:T(8,128)(2,1)} %reshape.203), kind=kLoop, calls=%fused_computation.12 | loop fusion | flops 1540096 | bytes 932864 | tf_op jit(solution)/shard_map/reduce_sum | solution.py:67
  97.4 0.0 all-gather.6.cloned.1.call-update
  97.5 1.8 broadcast_compare_fusion
  99.3 0.1 copy.72
  99.4 0.1 broadcast_compare_fusion.1
  99.5 0.0 copy-start.1
  99.5 0.1 copy.71
  99.6 102.9 %all-to-all-done = bf16[1,64,4,12,384]{4,2,3,0,1:T(4,128)(2,1)} async-done(((bf16[1,64,4,12,384]{4,2,3,0,1:T(4,128)(2,1)}), bf16[1,64,4,12,384]{4,2,3,0,1:T(4,128)(2,1)}, u32[]{:S(2)}, u32[]{:S(2)}) %all-to-all-start) | async-done | bytes 2359328 | tf_op jit(solution)/shard_map/all_to_all | solution.py:76
  202.5 3.3 fusion.16
  205.8 0.0 copy-done.1
  205.8 10.4 %fusion.17 = (f32[4,64,12]{1,2,0:T(8,128)S(1)}, f32[4,64,12,64,12]{1,3,4,2,0:T(8,128)}) fusion(bf16[1,64,4,12,128]{4,2,3,0,1:T(4,128)(2,1)S(1)} %get-tuple-element.4, bf16[1,64,4,12,128]{4,2,3,0,1:T(4,128)(2,1)S(1)} %get-tuple-element.3, pred[64,12,64,12]{0,2,3,1:T(8,128)(4,1)S(1)} %copy-done.1, s32[4,64,12]{1,2,0:T(8,128)S(1)} %copy.72, ...), kind=kOutput, calls=%fused_computation.48 | convolution fusion | flops 618132480 | bytes 11627520 | tf_op jit(solution)/shard_map/hscie,htcje->hcsitj/dot_general | solution.py:34
  216.2 0.0 copy-start.2
  216.2 10.3 %fusion = f32[4,64,12]{1,2,0:T(8,128)S(1)} fusion(f32[4,64,12,64,12]{1,3,4,2,0:T(8,128)} %get-tuple-element.9, f32[4,64,12]{1,2,0:T(8,128)S(1)} %get-tuple-element.8), kind=kLoop, calls=%fused_computation.5 | loop fusion | flops 4715520 | bytes 9461760 | tf_op jit(solution)/shard_map/reduce_sum | solution.py:44
  226.5 0.0 copy-done.2
  226.5 8.7 %fusion.6 = bf16[1,64,4,12,128]{4,1,3,2,0:T(8,128)(2,1)S(1)} fusion(f32[4,64,12,64,12]{1,3,4,2,0:T(8,128)} %get-tuple-element.9, f32[4,64,12]{1,2,0:T(8,128)S(1)} %fusion, f32[4,64,12]{1,2,0:T(8,128)S(1)} %get-tuple-element.8, bf16[1,64,4,12,128]{4,2,3,0,1:T(4,128)(2,1)S(1)} %copy-done.2), kind=kOutput, calls=%fused_computation.16 | convolution fusion | flops 611450880 | bytes 11034624 | tf_op jit(solution)/shard_map/hcsitj,htcje->hscie/dot_general | solution.py:45
  235.2 0.0 copy-start.4
  235.3 0.0 copy-start.5
  235.3 1.5 copy.77
  236.8 11.6 %all-to-all-start.2 = ((bf16[1,64,4,12,128]{4,2,3,0,1:T(4,128)(2,1)}), bf16[1,64,4,12,128]{4,2,3,0,1:T(4,128)(2,1)}, u32[]{:S(2)}, u32[]{:S(2)}) async-start(bf16[1,64,4,12,128]{4,2,3,0,1:T(4,128)(2,1)} %copy.77), calls=%async_computation.2 | async-start | bytes 1572864 | tf_op jit(solution)/shard_map/all_to_all | solution.py:79
  248.4 0.0 copy-done.4
  248.4 0.1 multiply_reduce_fusion
  248.6 0.0 copy-done.5
  248.6 0.1 and_reduce_fusion
  248.7 0.1 copy.64
  248.8 0.1 reshape.212
  248.9 51.4 %all-to-all-done.2 = bf16[1,64,4,12,128]{4,2,3,0,1:T(4,128)(2,1)} async-done(((bf16[1,64,4,12,128]{4,2,3,0,1:T(4,128)(2,1)}), bf16[1,64,4,12,128]{4,2,3,0,1:T(4,128)(2,1)}, u32[]{:S(2)}, u32[]{:S(2)}) %all-to-all-start.2) | async-done | bytes 786464 | tf_op jit(solution)/shard_map/all_to_all | solution.py:79
  300.3 1.4 copy.78
  301.8 1.1 reshape.214
  302.8 8.6 %scatter_custom_fusion = bf16[1024,128]{1,0:T(8,128)(2,1)S(1)} fusion(s32[3072]{0:T(1024)S(1)} %reshape.212, bf16[3072,128]{1,0:T(8,128)(2,1)} %reshape.214, bf16[]{:T(256)} %constant.15.clone.1), kind=kCustom, calls=%fused_computation.23 | custom fusion | bytes 262656
  311.4 0.5 broadcast.149
  312.0 0.8 reduce.17
  312.8 0.8 reshape.233
  313.5 6.0 %all-to-all-start.3 = ((bf16[8,2,8192]{2,1,0:T(2,128)(2,1)}), bf16[8,2,8192]{2,1,0:T(2,128)(2,1)S(1)}, u32[]{:S(2)}, u32[]{:S(2)}) async-start(bf16[8,2,8192]{2,1,0:T(2,128)(2,1)} %reshape.233), calls=%async_computation.3 | async-start | bytes 524288 | tf_op jit(solution)/shard_map/all_to_all | solution.py:90
  319.5 6.5 %all-to-all-done.3 = bf16[8,2,8192]{2,1,0:T(2,128)(2,1)S(1)} async-done(((bf16[8,2,8192]{2,1,0:T(2,128)(2,1)}), bf16[8,2,8192]{2,1,0:T(2,128)(2,1)S(1)}, u32[]{:S(2)}, u32[]{:S(2)}) %all-to-all-start.3) | async-done | bytes 262176 | tf_op jit(solution)/shard_map/all_to_all | solution.py:90
  326.0 0.3 reshape.234
  326.3 0.0 all-gather.4.cloned.1.call-done
  326.4 2.7 fusion.7
  329.1 0.0 all-gather.6.cloned.1.call-done
  329.1 3.8 %reduce.14 = f32[256,128]{1,0:T(8,128)S(1)} reduce(f32[64,256,128]{2,1,0:T(8,128)} %bitcast.73, f32[]{:T(128)} %constant.11.clone.1), dimensions={0}, to_apply=%region_5.6 | reduce | flops 2064384 | bytes 8519684 | tf_op jit(solution)/shard_map/reduce_sum | solution.py:11
  332.9 0.1 multiply_reduce_fusion.1
  333.0 0.7 multiply_bitcast_fusion
  (7 shorter events, 0.1 us)
Async XLA Ops:
  7.2 21.4 %copy-start = (bf16[1024,1024]{1,0:T(8,128)(2,1)S(1)}, bf16[1024,1024]{1,0:T(8,128)(2,1)}, u32[]{:S(2)}) copy-start(bf16[1024,1024]{1,0:T(8,128)(2,1)} %param.5) | copy-start | bytes 6291460
  7.2 319.2 %all-gather.4.cloned.1.call-start = ((), (), s32[]{:S(2)}) async-start(), calls=%async_computation.4 | async-start | bytes 2359296 | tf_op jit(solution)/shard_map/all_gather | solution.py:94
  9.4 62.3 %all-to-all-start.1 = ((s32[1,64,4,12]{3,2,0,1:T(4,128)}), s32[1,64,4,12]{3,2,0,1:T(4,128)S(1)}, u32[]{:S(2)}, u32[]{:S(2)}) async-start(s32[1,64,4,12]{3,2,0,1:T(4,128)} %bitcast.10), calls=%async_computation.1 | async-start | bytes 262144 | tf_op jit(solution)/shard_map/all_to_all | solution.py:77
  71.8 130.7 %all-to-all-start = ((bf16[1,64,4,12,384]{4,2,3,0,1:T(4,128)(2,1)}), bf16[1,64,4,12,384]{4,2,3,0,1:T(4,128)(2,1)}, u32[]{:S(2)}, u32[]{:S(2)}) async-start(bf16[1,64,4,12,384]{4,2,3,0,1:T(4,128)(2,1)} %copy.67), calls=%async_computation | async-start | bytes 4718592 | tf_op jit(solution)/shard_map/all_to_all | solution.py:76
  86.5 7.1 %copy-start.3 = (s32[1,1,256]{2,1,0:T(1,128)S(1)}, s32[1,1,256]{2,1,0:T(1,128)}, u32[]{:S(2)}) copy-start(s32[1,1,256]{2,1,0:T(1,128)} %param.9) | copy-start | bytes 3076
  86.5 242.6 %all-gather.6.cloned.1.call-start = ((), (), s32[]{:S(2)}) async-start(), calls=%async_computation.5 | async-start | bytes 8519680 | tf_op jit(solution)/shard_map/all_gather | solution.py:10
  99.5 106.4 %copy-start.1 = (pred[64,12,64,12]{0,2,3,1:T(8,128)(4,1)S(1)}, pred[64,12,64,12]{0,2,3,1:T(8,128)(4,1)}, u32[]{:S(2)}) copy-start(pred[64,12,64,12]{0,2,3,1:T(8,128)(4,1)} %broadcast_compare_fusion) | copy-start | bytes 1769476
  216.2 10.3 %copy-start.2 = (bf16[1,64,4,12,128]{4,2,3,0,1:T(4,128)(2,1)S(1)}, bf16[1,64,4,12,128]{4,2,3,0,1:T(4,128)(2,1)}, u32[]{:S(2)}) copy-start(bf16[1,64,4,12,128]{4,2,3,0,1:T(4,128)(2,1)} %get-tuple-element.2) | copy-start | bytes 2359300
  235.2 13.2 %copy-start.4 = (s32[2]{0:T(128)S(1)}, s32[2]{0:T(128)}, u32[]{:S(2)}) copy-start(s32[2]{0:T(128)} %constant.45) | copy-start | bytes 28
  235.3 13.3 %copy-start.5 = (s32[2]{0:T(128)S(1)}, s32[2]{0:T(128)}, u32[]{:S(2)}) copy-start(s32[2]{0:T(128)} %constant.48) | copy-start | bytes 28
  236.8 63.6 %all-to-all-start.2 = ((bf16[1,64,4,12,128]{4,2,3,0,1:T(4,128)(2,1)}), bf16[1,64,4,12,128]{4,2,3,0,1:T(4,128)(2,1)}, u32[]{:S(2)}, u32[]{:S(2)}) async-start(bf16[1,64,4,12,128]{4,2,3,0,1:T(4,128)(2,1)} %copy.77), calls=%async_computation.2 | async-start | bytes 1572864 | tf_op jit(solution)/shard_map/all_to_all | solution.py:79
  313.5 12.5 %all-to-all-start.3 = ((bf16[8,2,8192]{2,1,0:T(2,128)(2,1)}), bf16[8,2,8192]{2,1,0:T(2,128)(2,1)S(1)}, u32[]{:S(2)}, u32[]{:S(2)}) async-start(bf16[8,2,8192]{2,1,0:T(2,128)(2,1)} %reshape.233), calls=%async_computation.3 | async-start | bytes 524288 | tf_op jit(solution)/shard_map/all_to_all | solution.py:90
Sparse Core Ops, SparseCore 0:
  10.2 38.5 all-gather.3
  97.6 213.5 all-gather.5
